TPU v7x, 512 devices: a whole 4x4x16 slice. The times are simulated.
512 devices in a mesh: pix: 32 (over z_lo, y), mass: 16 (over z_hi, x, core).
Axes of the slice: x: 4, y: 4, z: 16 (z_hi: 2, z_lo: 8; z = z_hi * 8 + z_lo), core: 2. Of those that a mesh axis runs over, the one named last changes fastest.
Arguments:
- tiles: bfloat16 [32, 16, 16, 256, 256], P('pix', 'mass'), may hold values from 10 to 1000
- tile_pos: int32 [32, 16, 16], P('pix', 'mass'), may hold values from 0 to 255, as said below
- kept_tile_count: int32 [32, 16], P('pix', 'mass'), may hold values from 1 to 16, as said below
- loading: float32 [64, 65536], P('mass', 'pix'), may hold values from 0.006 to 6.5, as said below
- spectra: float32 [64, 131072], P('pix', 'mass'), may hold values from 0.006 to 6.5, as said below
Outputs:
- loading_new: float32 [64, 65536], P('mass', 'pix')
- spectra_new: float32 [64, 131072], P('pix', 'mass')
Inputs may be any that keep to these rules, and one draw needn't show every extreme that they name: `tile_pos`: on each device the 16 entries are distinct; entry q names tile row q // 32 and tile column q % 32 of the device's block. `kept_tile_count`: some device holds exactly 16 kept tiles. `loading`: every entry is positive. `spectra`: every entry is positive.
All inputs are finite; a program needn't handle non-finite values.
Results may differ from a plain program's by a relative error of at most 0.00065.
Values may be sent and summed in bfloat16 or wider, within the bound.
No kernel may reach another device: no remote copies, remote signals or barrier semaphores. Data moves between devices by JAX's collectives and lax.ppermute only.
A program may use at most 64 MiB of HBM per device.

v0:
```python
import jax
import jax.numpy as jnp
from jax import lax
from jax.sharding import PartitionSpec as P


def local(tiles, tile_pos, kept_tile_count, loading, spectra):
    largest_value = lax.Precision.HIGHEST
    stacked_tiles = tiles[0, 0]
    places = tile_pos[0, 0]
    kept_count = kept_tile_count[0, 0]
    slot_count = stacked_tiles.shape[0]
    tile_size = stacked_tiles.shape[1]
    mass_size = lax.axis_size("mass")
    rank_size = loading.shape[0] * mass_size
    pix_dev = loading.shape[1]
    bins_dev = spectra.shape[1]
    tile_rows = pix_dev // tile_size
    tile_cols = bins_dev // tile_size
    live_mask = (jnp.arange(slot_count) < kept_count).astype(jnp.float32)
    row_of = places // tile_cols
    col_of = places % tile_cols
    row_hot = (row_of[:, None] == jnp.arange(tile_rows)[None, :]).astype(jnp.float32) * live_mask[
        :, None
    ]
    column_onehot = (col_of[:, None] == jnp.arange(tile_cols)[None, :]).astype(
        jnp.float32
    ) * live_mask[:, None]
    whole_load = lax.all_gather(loading.astype(jnp.bfloat16), "mass", axis=0, tiled=True)
    gram_load = lax.psum(
        jnp.einsum("kp,jp->kj", whole_load, whole_load, preferred_element_type=jnp.float32), "pix"
    )
    selected_loading = jnp.take(whole_load.reshape(rank_size, tile_rows, tile_size), row_of, axis=1)
    spectra_matrix_product = jnp.einsum(
        "tco,com->ctm", selected_loading, stacked_tiles, preferred_element_type=jnp.float32
    )
    spectra_upper = jnp.einsum(
        "xo,xbm->bom", column_onehot, spectra_matrix_product, precision=largest_value
    ).reshape(rank_size, bins_dev)
    top_rows = lax.psum_scatter(spectra_upper, "pix", scatter_dimension=0, tiled=True)
    old_whole = lax.all_gather(spectra.astype(jnp.bfloat16), "pix", axis=0, tiled=True)
    spec_rows = spectra.shape[0]
    gram_rows = lax.dynamic_slice_in_dim(gram_load, lax.axis_index("pix") * spec_rows, spec_rows, 0)
    bottom_rows = jnp.dot(gram_rows, old_whole.astype(jnp.float32), precision=largest_value)
    spectra_new = spectra * top_rows / bottom_rows
    whole_spec = lax.all_gather(spectra_new.astype(jnp.bfloat16), "pix", axis=0, tiled=True)
    picked_spec = jnp.take(whole_spec.reshape(rank_size, tile_cols, tile_size), col_of, axis=1)
    load_product = jnp.einsum(
        "ksv,suv->sku", picked_spec, stacked_tiles, preferred_element_type=jnp.float32
    )
    load_top = jnp.einsum("sr,sku->kru", row_hot, load_product, precision=largest_value).reshape(
        rank_size, pix_dev
    )
    load_rows = loading.shape[0]
    gram_part = jnp.einsum("km,jm->kj", whole_spec, whole_spec, preferred_element_type=jnp.float32)
    top_mine = lax.psum_scatter(load_top, "mass", scatter_dimension=0, tiled=True)
    gram_spec = lax.psum(gram_part, "mass")
    gram_spec_rows = lax.dynamic_slice_in_dim(
        gram_spec, lax.axis_index("mass") * load_rows, load_rows, 0
    )
    load_bottom = jnp.dot(gram_spec_rows, whole_load.astype(jnp.float32), precision=largest_value)
    loading_new = loading * top_mine / load_bottom
    return (loading_new, spectra_new)


def solution(mesh):
    return jax.shard_map(
        local,
        mesh=mesh,
        in_specs=(
            P("pix", "mass", None, None, None),
            P("pix", "mass", None),
            P("pix", "mass"),
            P("mass", "pix"),
            P("pix", "mass"),
        ),
        out_specs=(P("mass", "pix"), P("pix", "mass")),
        check_vma=False,
    )
```

profile of v0, /device:TPU:1, one launch (start us, length us, event | category | flops | bytes accessed | tf_op | source)
XLA Modules:
  0.0 1191.5 jit_solution(17400756126792257851)
XLA Ops:
  7.2 1.6 convert_bitcast_fusion.1
  8.9 0.0 all-reduce.5.cloned.1.call-start
  9.6 0.8 convert_bitcast_fusion.2
  10.3 51.4 %all-gather = bf16[16,4,2048]{2,1,0:T(4,128)(2,1)S(1)} all-gather(bf16[1,4,2048]{2,1,0:T(4,128)(2,1)S(1)} %convert_bitcast_fusion.2), channel_id=1, replica_groups=mesh['pix'=32,'mass'=16] {'mass'}, dimensions={0}, use_global_device_ids=true | all-gather | bytes 278528 | tf_op jit(solution)/shard_map/all_gather | solution.py:29
  61.7 0.2 reshape.169
  62.0 0.7 fusion.29
  62.6 0.6 gather_fusion
  63.3 0.5 fusion.2
  63.8 2.3 fusion.6
  66.1 2.5 copy.19
  68.7 0.0 all-gather.8.cloned.1.call-start
  68.7 0.1 reshape.190
  68.8 1.3 dynamic-slice
  70.7 0.2 fusion.36
  70.9 203.7 %psum.14 = f32[64,64]{1,0:T(8,128)} all-reduce(f32[64,64]{1,0:T(8,128)S(1)} %fusion.36), channel_id=1, replica_groups=mesh['pix'=32,'mass'=16] {'pix'}, use_global_device_ids=true, to_apply=%region_1.2 | all-reduce | flops 4096 | bytes 32768 | tf_op jit(solution)/shard_map/psum | solution.py:30
  274.7 1.5 reshape.192
  276.1 399.9 %all-reduce.5.cloned.1.call-done = f32[64,8192]{1,0:T(8,128)} async-done(((f32[64,8192]{1,0:T(8,128)}), f32[64,8192]{1,0:T(8,128)}) %all-reduce.5.cloned.1.call-update) | async-done | bytes 2097168
  676.1 1.5 convolution_divide_fusion
  677.6 0.6 convert_bitcast_fusion
  678.3 221.1 %all-gather.8.cloned.1.call-done = bf16[32,2,8192]{2,1,0:T(2,128)(2,1)} async-done(((bf16[1,2,8192]{2,1,0:T(2,128)(2,1)}), bf16[32,2,8192]{2,1,0:T(2,128)(2,1)}) %all-gather.8.cloned.1.call-update) | async-done | bytes 1048592 | tf_op jit(solution)/shard_map/all_gather | solution.py:46
  899.5 1.7 reshape.171
  901.2 1.6 copy.17
  902.8 1.8 gather_fusion.1
  904.6 0.8 fusion
  905.4 1.3 fusion.4
  906.7 1.0 copy.20
  907.6 1.3 dynamic-slice.2
  909.6 1.5 reshape.194
  911.1 0.4 fusion.37
  911.5 131.7 %psum.15 = f32[64,64]{1,0:T(8,128)S(1)} all-reduce(f32[64,64]{1,0:T(8,128)S(1)} %fusion.37), channel_id=1, replica_groups=mesh['pix'=32,'mass'=16] {'mass'}, use_global_device_ids=true, to_apply=%region_3.4 | all-reduce | flops 4096 | bytes 32768 | tf_op jit(solution)/shard_map/psum | solution.py:57
  1043.2 140.1 %all-reduce.7.cloned.1.call-done = f32[64,2048]{1,0:T(8,128)} async-done(((f32[64,2048]{1,0:T(8,128)}), f32[64,2048]{1,0:T(8,128)}) %all-reduce.7.cloned.1.call-update) | async-done | bytes 524304
  1183.3 1.7 convolution_divide_fusion.1
  (21 shorter events, 0.3 us)
Async XLA Ops:
  7.2 56.1 %copy-start = (bf16[1,1,16,256,256]{4,3,2,1,0:T(8,128)(2,1)S(1)}, bf16[1,1,16,256,256]{4,3,2,1,0:T(8,128)(2,1)}, u32[]{:S(2)}) copy-start(bf16[1,1,16,256,256]{4,3,2,1,0:T(8,128)(2,1)} %param.5) | copy-start | bytes 6291460
  7.2 56.0 %copy-start.4 = (s32[1,1,16]{2,1,0:T(1,128)S(1)}, s32[1,1,16]{2,1,0:T(1,128)}, u32[]{:S(2)}) copy-start(s32[1,1,16]{2,1,0:T(1,128)} %param.6) | copy-start | bytes 196
  7.2 267.5 %all-gather.6.cloned.1.call-start = ((), (), s32[]{:S(2)}) async-start(), calls=%async_computation | async-start | bytes 1081344 | tf_op jit(solution)/shard_map/all_gather | solution.py:41
  8.9 667.2 %all-reduce.5.cloned.1.call-start = ((), (), s32[]{:S(2)}) async-start(), calls=%async_computation.2 | async-start | bytes 4194304
  68.7 607.4 %copy-start.1 = (f32[2,8192]{1,0:T(2,128)S(1)}, f32[2,8192]{1,0:T(2,128)}, u32[]{:S(2)}) copy-start(f32[2,8192]{1,0:T(2,128)} %param.9) | copy-start | bytes 196612
  68.7 830.8 %all-gather.8.cloned.1.call-start = ((), (), s32[]{:S(2)}) async-start(), calls=%async_computation.1 | async-start | bytes 1081344 | tf_op jit(solution)/shard_map/all_gather | solution.py:46
  677.6 225.2 %copy-start.2 = (f32[2,8192]{1,0:T(2,128)}, f32[2,8192]{1,0:T(2,128)S(1)}, u32[]{:S(2)}) copy-start(f32[2,8192]{1,0:T(2,128)S(1)} %convolution_divide_fusion) | copy-start | bytes 196612
  678.3 505.0 %all-reduce.7.cloned.1.call-start = ((), (), s32[]{:S(2)}) async-start(), calls=%async_computation.3 | async-start | bytes 1048576
  909.6 273.7 %copy-start.3 = (f32[4,2048]{1,0:T(4,128)S(1)}, f32[4,2048]{1,0:T(4,128)}, u32[]{:S(2)}) copy-start(f32[4,2048]{1,0:T(4,128)} %param.8) | copy-start | bytes 98308
Sparse Core Ops, SparseCore 0:
  10.7 205.9 all-gather.5
  219.6 456.4 all-reduce.4
  678.9 220.4 all-gather.7
  907.8 275.4 all-reduce.6
where the time goes:
time: 1190 us
  waiting for transfers between devices  761 us (64%)
  blocking collectives  387 us (33%)
  between operations  15.9 us (1%)
  local copies, waits for them, and re-layouts  15 us (1%)
    unnamed x6, waiting for transfers between devices  540 us
    all_gather x1, waiting for transfers between devices, local(): lax.all_gather(spectra_new.astype(jnp.bfloat16), 'pix', axis=0, tiled=True)  221 us
    psum x1, blocking collectives, local(): lax.psum(jnp.einsum('kp,jp->kj', whole_load, whole_load, preferred_elemen...  204 us
    psum x1, blocking collectives, local(): gram_spec = lax.psum(gram_part, 'mass')  132 us
    all_gather x1, blocking collectives, local(): lax.all_gather(loading.astype(jnp.bfloat16), 'mass', axis=0, tiled=True)  51.4 us
  transfers between devices with their start and end apart: 4, of which 3 were waited for; matrix products, arithmetic and copies ran while one was open for 1% of the time, Pallas kernels for 0%

commit v1 on v0

--- a/solution.py
+++ b/solution.py
@@ -43,7 +43,11 @@
     gram_rows = lax.dynamic_slice_in_dim(gram_load, lax.axis_index("pix") * spec_rows, spec_rows, 0)
     bottom_rows = jnp.dot(gram_rows, old_whole.astype(jnp.float32), precision=largest_value)
     spectra_new = spectra * top_rows / bottom_rows
-    whole_spec = lax.all_gather(spectra_new.astype(jnp.bfloat16), "pix", axis=0, tiled=True)
+    part = spectra_new.astype(jnp.bfloat16)
+    size = lax.axis_size("pix")
+    blocks = jnp.stack([part for _ in range(size)])
+    blocks = lax.all_to_all(blocks, "pix", split_axis=0, concat_axis=0)
+    whole_spec = jnp.concatenate(blocks, axis=0)
     picked_spec = jnp.take(whole_spec.reshape(rank_size, tile_cols, tile_size), col_of, axis=1)
     load_product = jnp.einsum(
         "ksv,suv->sku", picked_spec, stacked_tiles, preferred_element_type=jnp.float32

time: 1190 us -> 1010 us (0.85)
  waiting for transfers between devices: 761 us -> 563 us
    all_gather x1 -> x0, waiting for transfers between devices: 221 us -> none  [local(): lax.all_gather(spectra_new.astype(jnp.bfloat16), 'pix', axis=0, tiled=True)]
    all_to_all x0 -> x1, waiting for transfers between devices: none -> 28.7 us  [local(): blocks = lax.all_to_all(blocks, 'pix', split_axis=0, concat_axis=0)]
    unnamed x6 -> x5, waiting for transfers between devices: 540 us -> 535 us
where the time goes in v1:
time: 1010 us
  waiting for transfers between devices  563 us (56%)
  blocking collectives  390 us (39%)
  local copies, waits for them, and re-layouts  18.4 us (2%)
  between operations  15.9 us (2%)
  matrix products  11.9 us (1%)
  starting transfers between devices  10.9 us (1%)
    unnamed x5, waiting for transfers between devices  535 us
    psum x1, blocking collectives, local(): lax.psum(jnp.einsum('kp,jp->kj', whole_load, whole_load, preferred_elemen...  204 us
    psum x1, blocking collectives, local(): gram_spec = lax.psum(gram_part, 'mass')  134 us
    all_gather x1, blocking collectives, local(): lax.all_gather(loading.astype(jnp.bfloat16), 'mass', axis=0, tiled=True)  51.4 us
    all_to_all x1, waiting for transfers between devices, local(): blocks = lax.all_to_all(blocks, 'pix', split_axis=0, concat_axis=0)  28.7 us
  transfers between devices with their start and end apart: 4, of which 3 were waited for; matrix products, arithmetic and copies ran while one was open for 1% of the time, Pallas kernels for 0%

profile of v1, /device:TPU:1, one launch (start us, length us, event | category | flops | bytes accessed | tf_op | source)
XLA Modules:
  0.0 1013.0 jit_solution(10682885696897774421)
XLA Ops:
  7.2 1.6 convert_bitcast_fusion
  8.9 0.0 all-reduce.5.cloned.1.call-start
  9.6 0.8 convert_bitcast_fusion.1
  10.3 51.4 %all-gather = bf16[16,4,2048]{2,1,0:T(4,128)(2,1)S(1)} all-gather(bf16[1,4,2048]{2,1,0:T(4,128)(2,1)S(1)} %convert_bitcast_fusion.1), channel_id=1, replica_groups=mesh['pix'=32,'mass'=16] {'mass'}, dimensions={0}, use_global_device_ids=true | all-gather | bytes 278528 | tf_op jit(solution)/shard_map/all_gather | solution.py:29
  61.7 0.2 reshape.171
  62.0 0.7 fusion.29
  62.6 0.6 gather_fusion
  63.3 0.5 fusion.2
  63.8 2.3 fusion.6
  66.1 2.5 copy.15
  68.7 0.1 reshape.192
  68.8 1.3 dynamic-slice
  70.7 0.2 fusion.37
  70.9 203.9 %psum.14 = f32[64,64]{1,0:T(8,128)S(1)} all-reduce(f32[64,64]{1,0:T(8,128)S(1)} %fusion.37), channel_id=1, replica_groups=mesh['pix'=32,'mass'=16] {'pix'}, use_global_device_ids=true, to_apply=%region_1.2 | all-reduce | flops 4096 | bytes 32768 | tf_op jit(solution)/shard_map/psum | solution.py:30
  274.8 1.5 reshape.194
  276.2 399.7 %all-reduce.5.cloned.1.call-done = f32[64,8192]{1,0:T(8,128)} async-done(((f32[64,8192]{1,0:T(8,128)}), f32[64,8192]{1,0:T(8,128)}) %all-reduce.5.cloned.1.call-update) | async-done | bytes 2097168
  675.9 2.1 fusion.36
  678.1 1.9 stack.2
  680.0 10.7 %all-to-all-start = ((bf16[32,2,8192]{2,1,0:T(2,128)(2,1)}), bf16[32,2,8192]{2,1,0:T(2,128)(2,1)S(1)}, u32[]{:S(2)}, u32[]{:S(2)}) async-start(bf16[32,2,8192]{2,1,0:T(2,128)(2,1)} %stack.2), calls=%async_computation | async-start | bytes 2097152 | tf_op jit(solution)/shard_map/all_to_all | solution.py:49
  690.8 28.7 %all-to-all-done = bf16[32,2,8192]{2,1,0:T(2,128)(2,1)S(1)} async-done(((bf16[32,2,8192]{2,1,0:T(2,128)(2,1)}), bf16[32,2,8192]{2,1,0:T(2,128)(2,1)S(1)}, u32[]{:S(2)}, u32[]{:S(2)}) %all-to-all-start) | async-done | bytes 1048608 | tf_op jit(solution)/shard_map/all_to_all | solution.py:49
  719.5 1.5 reshape_reshape.3
  721.0 2.8 copy.13
  723.8 2.6 gather_fusion.1
  726.4 1.8 fusion
  728.2 1.3 fusion.4
  729.4 1.0 copy.16
  730.4 1.3 dynamic-slice.2
  732.4 1.2 reshape.174
  733.6 2.0 fusion.38
  735.6 134.3 %psum.15 = f32[64,64]{1,0:T(8,128)S(1)} all-reduce(f32[64,64]{1,0:T(8,128)S(1)} %fusion.38), channel_id=1, replica_groups=mesh['pix'=32,'mass'=16] {'mass'}, use_global_device_ids=true, to_apply=%region_3.4 | all-reduce | flops 4096 | bytes 32768 | tf_op jit(solution)/shard_map/psum | solution.py:61
  869.8 134.9 %all-reduce.7.cloned.1.call-done = f32[64,2048]{1,0:T(8,128)} async-done(((f32[64,2048]{1,0:T(8,128)}), f32[64,2048]{1,0:T(8,128)}) %all-reduce.7.cloned.1.call-update) | async-done | bytes 524304
  1004.8 1.7 convolution_divide_fusion.1
  (18 shorter events, 0.2 us)
Async XLA Ops:
  7.2 56.1 %copy-start = (bf16[1,1,16,256,256]{4,3,2,1,0:T(8,128)(2,1)S(1)}, bf16[1,1,16,256,256]{4,3,2,1,0:T(8,128)(2,1)}, u32[]{:S(2)}) copy-start(bf16[1,1,16,256,256]{4,3,2,1,0:T(8,128)(2,1)} %param.5) | copy-start | bytes 6291460
  7.2 56.0 %copy-start.3 = (s32[1,1,16]{2,1,0:T(1,128)S(1)}, s32[1,1,16]{2,1,0:T(1,128)}, u32[]{:S(2)}) copy-start(s32[1,1,16]{2,1,0:T(1,128)} %param.6) | copy-start | bytes 196
  7.2 267.6 %all-gather.4.cloned.1.call-start = ((), (), s32[]{:S(2)}) async-start(), calls=%async_computation.1 | async-start | bytes 1081344 | tf_op jit(solution)/shard_map/all_gather | solution.py:41
  8.9 667.1 %all-reduce.5.cloned.1.call-start = ((), (), s32[]{:S(2)}) async-start(), calls=%async_computation.2 | async-start | bytes 4194304
  68.7 607.3 %copy-start.1 = (f32[2,8192]{1,0:T(2,128)S(1)}, f32[2,8192]{1,0:T(2,128)}, u32[]{:S(2)}) copy-start(f32[2,8192]{1,0:T(2,128)} %param.9) | copy-start | bytes 196612
  680.0 39.5 %all-to-all-start = ((bf16[32,2,8192]{2,1,0:T(2,128)(2,1)}), bf16[32,2,8192]{2,1,0:T(2,128)(2,1)S(1)}, u32[]{:S(2)}, u32[]{:S(2)}) async-start(bf16[32,2,8192]{2,1,0:T(2,128)(2,1)} %stack.2), calls=%async_computation | async-start | bytes 2097152 | tf_op jit(solution)/shard_map/all_to_all | solution.py:49
  690.7 314.1 %all-reduce.7.cloned.1.call-start = ((), (), s32[]{:S(2)}) async-start(), calls=%async_computation.3 | async-start | bytes 1048576
  732.3 272.5 %copy-start.2 = (f32[4,2048]{1,0:T(4,128)S(1)}, f32[4,2048]{1,0:T(4,128)}, u32[]{:S(2)}) copy-start(f32[4,2048]{1,0:T(4,128)} %param.8) | copy-start | bytes 98308
Sparse Core Ops, SparseCore 0:
  10.7 205.9 all-gather.3
  219.6 456.3 all-reduce.4
  730.5 274.2 all-reduce.6
